TPU v7x, 32 devices: a whole 2x2x4 slice. The times are simulated.
32 devices in a mesh: fsdp: 8 (over z, y), ctx: 2 (over x), tp: 2 (over core).
Axes of the slice: x: 2, y: 2, z: 4, core: 2. Of those that a mesh axis runs over, the one named last changes fastest.
Arguments:
- tokens_in: bfloat16 [4096, 2048], P(('fsdp', 'ctx')), may hold values from -6 to 6
- doc_positions: int32 [4096], P(('fsdp', 'ctx')), may hold values from 0 to 383, as said below
- attn_gain: bfloat16 [2048], P('fsdp'), may hold values from 0.25 to 1.75
- query_weight: bfloat16 [2048, 2048], P('fsdp', 'tp'), may hold values from -1 to 1
- key_weight: bfloat16 [2048, 256], P('fsdp', 'tp'), may hold values from -1 to 1
- value_weight: bfloat16 [2048, 256], P('fsdp', 'tp'), may hold values from -0.125 to 0.125
- output_weight: bfloat16 [2048, 2048], P('fsdp', 'tp'), may hold values from -2 to 2
- mlp_gain: bfloat16 [2048], P('fsdp'), may hold values from 0.25 to 1.75
- gate_weight: bfloat16 [2048, 5632], P('fsdp', 'tp'), may hold values from -0.125 to 0.125
- up_weight: bfloat16 [2048, 5632], P('fsdp', 'tp'), may hold values from -0.125 to 0.125
- down_weight: bfloat16 [2048, 5632], P('fsdp', 'tp'), may hold values from -0.078125 to 0.078125
- cotangent: bfloat16 [4096, 2048], P(('fsdp', 'ctx')), may hold values from -6 to 6
Outputs:
- block_out: bfloat16 [4096, 2048], P(('fsdp', 'ctx'))
- grad_tokens: float32 [4096, 2048], P(('fsdp', 'ctx'))
- grad_attn_gain: float32 [2048], P('fsdp')
- grad_query: float32 [2048, 2048], P('fsdp', 'tp')
- grad_key: float32 [2048, 256], P('fsdp', 'tp')
- grad_value: float32 [2048, 256], P('fsdp', 'tp')
- grad_output: float32 [2048, 2048], P('fsdp', 'tp')
- grad_mlp_gain: float32 [2048], P('fsdp')
- grad_gate: float32 [2048, 5632], P('fsdp', 'tp')
- grad_up: float32 [2048, 5632], P('fsdp', 'tp')
- grad_down: float32 [2048, 5632], P('fsdp', 'tp')
Inputs may be any that keep to these rules, and one draw needn't show every extreme that they name: `doc_positions`: each sequence of 512 tokens is packed with documents and begins with a new one; a token's value is its offset within its document: 0 at a document's first token, rising by one along it. Documents hold 102 to 384 tokens, except that the last of a sequence may be cut short; some document holds exactly 384.
All inputs are finite; a program needn't handle non-finite values.
Results may differ from a plain program's by a relative error of at most 0.014.
The roundings to bfloat16 on the way count: a program that leaves them out, or rounds other values in their place, can miss the bound.
Values may be sent and summed in bfloat16 or wider, within the bound.
No kernel may reach another device: no remote copies, remote signals or barrier semaphores. Data moves between devices by JAX's collectives and lax.ppermute only.
A program may use at most 256 MiB of HBM per device.

v0:
```python
import jax
import jax.numpy as jnp
from jax import lax
from jax.sharding import PartitionSpec as P

HEADS = 32
KV_HEADS = 4
HEAD_DIM = 64
EPSILON = 1e-05
NEG_FILL = -1e30


def rotary_tables(positions):
    half_dim = HEAD_DIM // 2
    inverse = 1.0 / 10000.0 ** (jnp.arange(half_dim, dtype=jnp.float32) * (2.0 / HEAD_DIM))
    angles = positions.astype(jnp.float32)[:, None] * inverse[None, :]
    cosine_table = jnp.concatenate([jnp.cos(angles), jnp.cos(angles)], axis=-1)[:, None, :]
    sine_table = jnp.concatenate([jnp.sin(angles), jnp.sin(angles)], axis=-1)[:, None, :]
    return (cosine_table, sine_table)


def apply_rotary(values, cosine_table, sine_table):
    half_dim = values.shape[-1] // 2
    turned = jnp.concatenate([-values[..., half_dim:], values[..., :half_dim]], axis=-1)
    return values * cosine_table + turned * sine_table


def undo_rotary(gradient, cosine_table, sine_table):
    half_dim = gradient.shape[-1] // 2
    sined = gradient * sine_table
    return gradient * cosine_table + jnp.concatenate(
        [sined[..., half_dim:], -sined[..., :half_dim]], axis=-1
    )


def contract_last(left_array, right_array):
    return lax.dot_general(
        left_array, right_array, (((1,), (1,)), ((), ())), preferred_element_type=jnp.float32
    )


def contract_first(left_array, right_array):
    return lax.dot_general(
        left_array, right_array, (((0,), (0,)), ((), ())), preferred_element_type=jnp.float32
    )


def normed_fold(scaled, pieces):
    gain_float = pieces[0].astype(jnp.float32)
    normed = (scaled * gain_float[None, :]).astype(jnp.bfloat16)
    sums = tuple(
        (jnp.dot(normed, matrix, preferred_element_type=jnp.float32) for matrix in pieces[1:])
    )
    return sums + (normed, gain_float)


def row_fold(left_array, shard_piece):
    return jnp.dot(left_array, shard_piece, preferred_element_type=jnp.float32)


def column_fold(gradients_in, pieces):
    part_sum = contract_last(gradients_in[0], pieces[0])
    for grad_piece, weight_piece in zip(gradients_in[1:], pieces[1:]):
        part_sum = part_sum + contract_last(grad_piece, weight_piece)
    return part_sum


def column_map(left_array, shard_piece):
    return contract_last(left_array, shard_piece)


def tensor_total(partial_sum):
    return lax.psum(partial_sum, "tp")


def body(
    tokens_in,
    doc_positions,
    attn_gain,
    query_weight,
    key_weight,
    value_weight,
    output_weight,
    mlp_gain,
    gate_weight,
    up_weight,
    down_weight,
    cotangent,
):
    local_rows = tokens_in.shape[0]
    query_columns = query_weight.shape[1]
    key_columns = key_weight.shape[1]
    local_groups = key_columns // HEAD_DIM
    group_size = HEADS // KV_HEADS
    group_width = group_size * HEAD_DIM
    score_scale = HEAD_DIM ** (-0.5)
    tokens = tokens_in.astype(jnp.float32)
    rms_one = lax.rsqrt(jnp.mean(tokens * tokens, axis=-1, keepdims=True) + EPSILON)
    scaled_one = tokens * rms_one
    query_lin, key_lin, value_lin, normed_one, gain_one = normed_fold(
        scaled_one,
        (
            lax.all_gather(attn_gain, "fsdp", axis=0, tiled=True),
            lax.all_gather(query_weight, "fsdp", axis=0, tiled=True),
            lax.all_gather(key_weight, "fsdp", axis=0, tiled=True),
            lax.all_gather(value_weight, "fsdp", axis=0, tiled=True),
        ),
    )
    cosine_table, sine_table = rotary_tables(doc_positions)
    queries = (
        apply_rotary(query_lin.reshape(local_rows, -1, HEAD_DIM), cosine_table, sine_table)
        .astype(jnp.bfloat16)
        .reshape(local_rows, query_columns)
    )
    keys_low = (
        apply_rotary(key_lin.reshape(local_rows, -1, HEAD_DIM), cosine_table, sine_table)
        .astype(jnp.bfloat16)
        .reshape(local_rows, key_columns)
    )
    values_low = value_lin.astype(jnp.bfloat16)
    key_all, value_all = (
        lax.all_gather(keys_low, "ctx", axis=0, tiled=True),
        lax.all_gather(values_low, "ctx", axis=0, tiled=True),
    )
    key_count = key_all.shape[0]
    query_places = lax.axis_index("ctx") * local_rows + jnp.arange(local_rows, dtype=jnp.int32)
    key_places = jnp.arange(key_count, dtype=jnp.int32)
    allowed = (key_places[None, :] <= query_places[:, None]) & (
        key_places[None, :] >= (query_places - doc_positions)[:, None]
    )

    def head_scores(query_group, key_head):
        raw_scores = (
            jnp.einsum("ngd,kd->gnk", query_group, key_head, preferred_element_type=jnp.float32)
            * score_scale
        )
        return jnp.where(allowed[None], raw_scores, NEG_FILL)

    attended_parts = []
    lse_parts = []
    for group_index in range(local_groups):
        query_group = queries[
            :, group_index * group_width : (group_index + 1) * group_width
        ].reshape(local_rows, group_size, HEAD_DIM)
        key_head = key_all[:, group_index * HEAD_DIM : (group_index + 1) * HEAD_DIM]
        value_head = value_all[:, group_index * HEAD_DIM : (group_index + 1) * HEAD_DIM]
        scores = head_scores(query_group, key_head)
        largest = jnp.max(scores, axis=-1, keepdims=True)
        exponent = jnp.exp(scores - largest)
        totals = jnp.sum(exponent, axis=-1, keepdims=True)
        probs_low = (exponent / totals).astype(jnp.bfloat16)
        attended_parts.append(
            jnp.einsum(
                "gnk,kd->ngd", probs_low, value_head, preferred_element_type=jnp.float32
            ).reshape(local_rows, group_width)
        )
        lse_parts.append(largest + jnp.log(totals))
    attended_low = jnp.concatenate(attended_parts, axis=1).astype(jnp.bfloat16)
    attn_branch = tensor_total(
        column_map(attended_low, lax.all_gather(output_weight, "fsdp", axis=0, tiled=True))
    )
    residual = tokens + attn_branch
    rms_two = lax.rsqrt(jnp.mean(residual * residual, axis=-1, keepdims=True) + EPSILON)
    scaled_two = residual * rms_two
    gate_lin, up_lin, normed_two, gain_two = normed_fold(
        scaled_two,
        (
            lax.all_gather(mlp_gain, "fsdp", axis=0, tiled=True),
            lax.all_gather(gate_weight, "fsdp", axis=0, tiled=True),
            lax.all_gather(up_weight, "fsdp", axis=0, tiled=True),
        ),
    )
    silu_value = gate_lin / (1.0 + jnp.exp(-gate_lin))
    act_low = (silu_value * up_lin).astype(jnp.bfloat16)
    mlp_branch = tensor_total(
        column_map(act_low, lax.all_gather(down_weight, "fsdp", axis=0, tiled=True))
    )
    block_out = (residual + mlp_branch).astype(jnp.bfloat16)
    grad_out = cotangent.astype(jnp.float32)
    grad_act = row_fold(cotangent, lax.all_gather(down_weight, "fsdp", axis=0, tiled=True))
    sigmoid = 1.0 / (1.0 + jnp.exp(-gate_lin))
    grad_gate_lin = (grad_act * up_lin * sigmoid * (1.0 + gate_lin * (1.0 - sigmoid))).astype(
        jnp.bfloat16
    )
    grad_up_lin = (grad_act * silu_value).astype(jnp.bfloat16)
    grad_normed_two = tensor_total(
        column_fold(
            (grad_gate_lin, grad_up_lin),
            (
                lax.all_gather(gate_weight, "fsdp", axis=0, tiled=True),
                lax.all_gather(up_weight, "fsdp", axis=0, tiled=True),
            ),
        )
    )
    scaled_grad_two = grad_normed_two * gain_two[None, :]
    grad_residual = (
        grad_out
        + rms_two * scaled_grad_two
        - residual
        * (rms_two * rms_two * rms_two)
        * jnp.mean(scaled_grad_two * residual, axis=-1, keepdims=True)
    )
    grad_attn_low = grad_residual.astype(jnp.bfloat16)
    grad_attended = row_fold(
        grad_attn_low, lax.all_gather(output_weight, "fsdp", axis=0, tiled=True)
    ).astype(jnp.bfloat16)
    query_grads = []
    key_grads = []
    value_grads = []
    for group_index in range(local_groups):
        query_group = queries[
            :, group_index * group_width : (group_index + 1) * group_width
        ].reshape(local_rows, group_size, HEAD_DIM)
        key_head = key_all[:, group_index * HEAD_DIM : (group_index + 1) * HEAD_DIM]
        value_head = value_all[:, group_index * HEAD_DIM : (group_index + 1) * HEAD_DIM]
        probabilities = jnp.exp(head_scores(query_group, key_head) - lse_parts[group_index])
        probs_low = probabilities.astype(jnp.bfloat16)
        grad_group = grad_attended[
            :, group_index * group_width : (group_index + 1) * group_width
        ].reshape(local_rows, group_size, HEAD_DIM)
        grad_probs = jnp.einsum(
            "ngd,kd->gnk", grad_group, value_head, preferred_element_type=jnp.float32
        )
        row_dot = jnp.sum(probabilities * grad_probs, axis=-1, keepdims=True)
        grad_scores = (probabilities * (grad_probs - row_dot)).astype(jnp.bfloat16)
        query_grads.append(
            jnp.einsum("gnk,kd->ngd", grad_scores, key_head, preferred_element_type=jnp.float32)
            * score_scale
        )
        key_grads.append(
            jnp.einsum("gnk,ngd->kd", grad_scores, query_group, preferred_element_type=jnp.float32)
            * score_scale
        )
        value_grads.append(
            jnp.einsum("gnk,ngd->kd", probs_low, grad_group, preferred_element_type=jnp.float32)
        )
    key_grad_local, value_grad_local = (
        lax.psum_scatter(
            jnp.concatenate(key_grads, axis=1), "ctx", scatter_dimension=0, tiled=True
        ),
        lax.psum_scatter(
            jnp.concatenate(value_grads, axis=1), "ctx", scatter_dimension=0, tiled=True
        ),
    )
    grad_q_lin = (
        undo_rotary(jnp.concatenate(query_grads, axis=1), cosine_table, sine_table)
        .astype(jnp.bfloat16)
        .reshape(local_rows, query_columns)
    )
    grad_k_lin = (
        undo_rotary(key_grad_local.reshape(local_rows, -1, HEAD_DIM), cosine_table, sine_table)
        .astype(jnp.bfloat16)
        .reshape(local_rows, key_columns)
    )
    grad_v_lin = value_grad_local.astype(jnp.bfloat16)
    grad_normed_one = tensor_total(
        column_fold(
            (grad_q_lin, grad_k_lin, grad_v_lin),
            (
                lax.all_gather(query_weight, "fsdp", axis=0, tiled=True),
                lax.all_gather(key_weight, "fsdp", axis=0, tiled=True),
                lax.all_gather(value_weight, "fsdp", axis=0, tiled=True),
            ),
        )
    )
    scaled_grad_one = grad_normed_one * gain_one[None, :]
    grad_tokens = (
        grad_residual
        + rms_one * scaled_grad_one
        - tokens
        * (rms_one * rms_one * rms_one)
        * jnp.mean(scaled_grad_one * tokens, axis=-1, keepdims=True)
    )
    owned = lax.psum_scatter(
        (
            jnp.sum(grad_normed_one * scaled_one, axis=0),
            contract_first(normed_one, grad_q_lin),
            contract_first(normed_one, grad_k_lin),
            contract_first(normed_one, grad_v_lin),
            contract_first(grad_attn_low, attended_low),
            jnp.sum(grad_normed_two * scaled_two, axis=0),
            contract_first(normed_two, grad_gate_lin),
            contract_first(normed_two, grad_up_lin),
            contract_first(cotangent, act_low),
        ),
        "fsdp",
        scatter_dimension=0,
        tiled=True,
    )
    (
        gain_one_grad,
        query_grad,
        key_grad,
        value_grad,
        output_grad,
        gain_two_grad,
        gate_grad,
        up_grad,
        down_grad,
    ) = owned
    summed = lax.psum(
        (
            gain_one_grad,
            query_grad,
            key_grad,
            value_grad,
            output_grad,
            gain_two_grad,
            gate_grad,
            up_grad,
            down_grad,
        ),
        "ctx",
    )
    return (
        block_out,
        grad_tokens,
        summed[0],
        summed[1],
        summed[2],
        summed[3],
        summed[4],
        summed[5],
        summed[6],
        summed[7],
        summed[8],
    )


def solution(mesh):
    return jax.shard_map(
        body,
        mesh=mesh,
        in_specs=(
            P(("fsdp", "ctx"), None),
            P(("fsdp", "ctx")),
            P("fsdp"),
            P("fsdp", "tp"),
            P("fsdp", "tp"),
            P("fsdp", "tp"),
            P("fsdp", "tp"),
            P("fsdp"),
            P("fsdp", "tp"),
            P("fsdp", "tp"),
            P("fsdp", "tp"),
            P(("fsdp", "ctx"), None),
        ),
        out_specs=(
            P(("fsdp", "ctx"), None),
            P(("fsdp", "ctx"), None),
            P("fsdp"),
            P("fsdp", "tp"),
            P("fsdp", "tp"),
            P("fsdp", "tp"),
            P("fsdp", "tp"),
            P("fsdp"),
            P("fsdp", "tp"),
            P("fsdp", "tp"),
            P("fsdp", "tp"),
        ),
        check_vma=False,
    )
```

profile of v0, /device:TPU:0, one launch (start us, length us, event | category | flops | bytes accessed | tf_op | source)
XLA Modules:
  0.0 2660.1 jit_solution(7111655742602666391)
XLA Ops:
  9.4 22.6 all-gather
  35.1 33.7 %all_gather.43 = bf16[2048,128]{1,0:T(8,128)(2,1)S(1)} all-gather(bf16[256,128]{1,0:T(8,128)(2,1)S(1)} %copy-done.46), channel_id=1, replica_groups=mesh['fsdp'=8,'ctx'=2,'tp'=2] {'fsdp'}, dimensions={0}, use_global_device_ids=true | all-gather | bytes 589824 | tf_op jit(solution)/shard_map/all_gather | solution.py:105
  70.0 5.0 all_gather.44
  75.1 32.7 %all_gather.41 = bf16[2048,128]{1,0:T(8,128)(2,1)S(1)} all-gather(bf16[256,128]{1,0:T(8,128)(2,1)S(1)} %copy-done.47), channel_id=1, replica_groups=mesh['fsdp'=8,'ctx'=2,'tp'=2] {'fsdp'}, dimensions={0}, use_global_device_ids=true | all-gather | bytes 589824 | tf_op jit(solution)/shard_map/all_gather | solution.py:106
  131.4 39.2 %all-gather.10.cloned.1.call-done = bf16[2048,1024]{1,0:T(8,128)(2,1)} async-done(((bf16[256,1024]{1,0:T(8,128)(2,1)}), bf16[2048,1024]{1,0:T(8,128)(2,1)}) %all-gather.10.cloned.1.call-update) | async-done | bytes 4194320 | tf_op jit(solution)/shard_map/all_gather | solution.py:160
  177.3 18.3 all-gather.1
  200.0 162.1 %all-gather.14.cloned.1.call-done = bf16[2048,2816]{1,0:T(8,128)(2,1)} async-done(((bf16[256,2816]{1,0:T(8,128)(2,1)}), bf16[2048,2816]{1,0:T(8,128)(2,1)}) %all-gather.14.cloned.1.call-update) | async-done | bytes 11534352 | tf_op jit(solution)/shard_map/all_gather | solution.py:170
  362.1 9.3 fusion.74
  371.4 154.2 %all-gather.12.cloned.1.call-done = bf16[2048,2816]{1,0:T(8,128)(2,1)} async-done(((bf16[256,2816]{1,0:T(8,128)(2,1)}), bf16[2048,2816]{1,0:T(8,128)(2,1)}) %all-gather.12.cloned.1.call-update) | async-done | bytes 11534352 | tf_op jit(solution)/shard_map/all_gather | solution.py:169
  525.6 9.3 fusion.73
  534.9 154.2 %all-gather.16.cloned.1.call-done = bf16[2048,2816]{1,0:T(8,128)(2,1)} async-done(((bf16[256,2816]{1,0:T(8,128)(2,1)}), bf16[2048,2816]{1,0:T(8,128)(2,1)}) %all-gather.16.cloned.1.call-update) | async-done | bytes 11534352 | tf_op jit(solution)/shard_map/all_gather | solution.py:176
  689.2 11.1 multiply_convert_fusion
  700.3 7.1 fusion.76
  707.4 8.8 convolution_add_fusion.2
  718.9 16.9 all-reduce.13.cloned.1.call-done
  777.8 11.7 reduce-scatter.10.cloned.1.call-done
  793.0 6.3 fusion.40
  809.2 12.6 convolution_bitcast_fusion
  821.8 12.6 fusion.79
  834.7 12.6 fusion.78
  847.5 9.4 fusion.75
  861.1 63.5 %reduce-scatter.16.cloned.1.call-done = f32[256,128]{1,0:T(8,128)} async-done(((f32[2048,128]{1,0:T(8,128)}), f32[256,128]{1,0:T(8,128)}) %reduce-scatter.16.cloned.1.call-update) | async-done | bytes 131088 | tf_op jit(solution)/shard_map/reduce_scatter | solution.py:274
  924.6 149.9 %reduce-scatter.20.cloned.1.call-done = f32[256,1024]{1,0:T(8,128)} async-done(((f32[2048,1024]{1,0:T(8,128)}), f32[256,1024]{1,0:T(8,128)}) %reduce-scatter.20.cloned.1.call-update) | async-done | bytes 1048592 | tf_op jit(solution)/shard_map/reduce_scatter | solution.py:274
  1074.5 150.2 %reduce-scatter.14.cloned.1.call-done = f32[256,1024]{1,0:T(8,128)} async-done(((f32[2048,1024]{1,0:T(8,128)}), f32[256,1024]{1,0:T(8,128)}) %reduce-scatter.14.cloned.1.call-update) | async-done | bytes 1048592 | tf_op jit(solution)/shard_map/reduce_scatter | solution.py:274
  1224.8 376.5 %reduce-scatter.26.cloned.1.call-done = f32[256,2816]{0,1:T(8,128)} async-done(((f32[2048,2816]{0,1:T(8,128)}), f32[256,2816]{0,1:T(8,128)}) %reduce-scatter.26.cloned.1.call-update) | async-done | bytes 2883600 | tf_op jit(solution)/shard_map/reduce_scatter | solution.py:274
  1601.3 375.6 %reduce-scatter.24.cloned.1.call-done = f32[256,2816]{1,0:T(8,128)} async-done(((f32[2048,2816]{1,0:T(8,128)}), f32[256,2816]{1,0:T(8,128)}) %reduce-scatter.24.cloned.1.call-update) | async-done | bytes 2883600 | tf_op jit(solution)/shard_map/reduce_scatter | solution.py:274
  1976.9 375.6 %reduce-scatter.22.cloned.1.call-done = f32[256,2816]{1,0:T(8,128)} async-done(((f32[2048,2816]{1,0:T(8,128)}), f32[256,2816]{1,0:T(8,128)}) %reduce-scatter.22.cloned.1.call-update) | async-done | bytes 2883600 | tf_op jit(solution)/shard_map/reduce_scatter | solution.py:274
  2354.5 28.6 %all-reduce.15.cloned.1.call-done = (f32[256,2048]{1,0:T(8,128)}, f32[256,2048]{1,0:T(8,128)}) async-done(((f32[256,2048]{1,0:T(8,128)}, f32[256,2048]{1,0:T(8,128)}), (f32[256,2048]{1,0:T(8,128)}, f32[256,2048]{1,0:T(8,128)})) %all-reduce.15.cloned.1.call-update) | async-done | bytes 4194320 | tf_op jit(solution)/shard_map/psum | solution.py:73
  2385.3 37.3 %all-reduce.2 = (f32[2048]{0:T(1024)S(1)}, f32[2048]{0:T(1024)S(1)}) all-reduce(f32[2048]{0:T(1024)S(1)} %get-tuple-element.46, f32[2048]{0:T(1024)S(1)} %copy-done.52), channel_id=4, replica_groups=mesh['fsdp'=8,'ctx'=2,'tp'=2] {'fsdp'}, use_global_device_ids=true, to_apply=%region_17.18.clone | all-reduce | flops 4096 | bytes 32768
  2422.8 5.7 all-reduce.4
  2428.5 5.1 fusion.21
  2433.6 208.2 %all-reduce.17.cloned.1.call-done = (f32[256,1024]{1,0:T(8,128)}, f32[256,128]{1,0:T(8,128)}, f32[256,128]{1,0:T(8,128)}, f32[256,1024]{1,0:T(8,128)}, f32[256,2...) async-done(((f32[256,1024]{1,0:T(8,128)}, f32[256,128]{1,0:T(8,128)}, f32[256,128]{1,0:T(8,128)}, f32[256,1024]{1,0:T(8,128)}, f32[256,2816]{1,0:T(8,128)}, ...) | async-done | bytes 11010064 | tf_op jit(solution)/shard_map/psum | solution.py:301
  (251 shorter events, 117.9 us)
Async XLA Ops:
  7.2 61.7 %copy-start.5 = (bf16[256,2048]{1,0:T(8,128)(2,1)S(1)}, bf16[256,2048]{1,0:T(8,128)(2,1)}, u32[]{:S(2)}) copy-start(bf16[256,2048]{1,0:T(8,128)(2,1)} %param.12) | copy-start | bytes 3145732
  7.2 28.0 %copy-start.46 = (bf16[256,128]{1,0:T(8,128)(2,1)S(1)}, bf16[256,128]{1,0:T(8,128)(2,1)}, u32[]{:S(2)}) copy-start(bf16[256,128]{1,0:T(8,128)(2,1)} %param.16) | copy-start | bytes 196612
  7.2 106.9 %all-gather.8.cloned.1.call-start = ((), (), s32[]{:S(2)}) async-start(), calls=%async_computation.9 | async-start | bytes 4718592 | tf_op jit(solution)/shard_map/all_gather | solution.py:104
  7.9 162.7 %all-gather.10.cloned.1.call-start = ((), (), s32[]{:S(2)}) async-start(), calls=%async_computation.10 | async-start | bytes 4718592 | tf_op jit(solution)/shard_map/all_gather | solution.py:160
  8.7 187.0 %all-reduce.11.cloned.1.call-start = ((), (), s32[]{:S(2)}) async-start(), calls=%async_computation.11 | async-start | bytes 4194304 | tf_op jit(solution)/shard_map/psum | solution.py:73
  35.1 79.0 %copy-start.48 = (f32[256]{0:T(256)}, f32[256]{0:T(256)S(1)}, u32[]{:S(2)}) copy-start(f32[256]{0:T(256)S(1)} %get-tuple-element.83) | copy-start | bytes 3076
  107.8 6.3 copy-start.21
  130.6 40.1 %copy-start.37 = (bf16[64,8,256]{2,0,1:T(8,128)(2,1)}, bf16[64,8,256]{2,0,1:T(8,128)(2,1)S(1)}, u32[]{:S(2)}) copy-start(bf16[64,8,256]{2,0,1:T(8,128)(2,1)S(1)} %fusion.29) | copy-start | bytes 786436
  131.4 44.1 %copy-start.38 = (bf16[64,8,256]{2,0,1:T(8,128)(2,1)}, bf16[64,8,256]{2,0,1:T(8,128)(2,1)S(1)}, u32[]{:S(2)}) copy-start(bf16[64,8,256]{2,0,1:T(8,128)(2,1)S(1)} %fusion.30) | copy-start | bytes 786436
  175.5 186.5 %all-gather.14.cloned.1.call-start = ((), (), s32[]{:S(2)}) async-start(), calls=%async_computation.13 | async-start | bytes 12976128 | tf_op jit(solution)/shard_map/all_gather | solution.py:170
  176.1 349.5 %all-gather.12.cloned.1.call-start = ((), (), s32[]{:S(2)}) async-start(), calls=%async_computation.12 | async-start | bytes 12976128 | tf_op jit(solution)/shard_map/all_gather | solution.py:169
  176.7 512.5 %all-gather.16.cloned.1.call-start = ((), (), s32[]{:S(2)}) async-start(), calls=%async_computation.14 | async-start | bytes 12976128 | tf_op jit(solution)/shard_map/all_gather | solution.py:176
  177.3 558.6 %all-reduce.13.cloned.1.call-start = ((), (), s32[]{:S(2)}) async-start(), calls=%async_computation.15 | async-start | bytes 4194304 | tf_op jit(solution)/shard_map/psum | solution.py:73
  700.3 7.1 copy-start.25
  700.3 7.1 copy-start.26
  716.2 58.7 %reduce-scatter.12.cloned.1.call-start = ((), (), s32[]{:S(2)}) async-start(), calls=%async_computation.17 | async-start | bytes 393216 | tf_op jit(solution)/shard_map/reduce_scatter | solution.py:241
  761.8 27.7 %reduce-scatter.10.cloned.1.call-start = ((), (), s32[]{:S(2)}) async-start(), calls=%async_computation.16 | async-start | bytes 393216 | tf_op jit(solution)/shard_map/reduce_scatter | solution.py:238
  761.9 6.7 copy-start.10
  761.9 6.7 copy-start.53
  771.8 89.3 %reduce-scatter.18.cloned.1.call-start = ((), (), s32[]{:S(2)}) async-start(), calls=%async_computation.20 | async-start | bytes 1179648 | tf_op jit(solution)/shard_map/reduce_scatter | solution.py:274
  777.4 147.2 %reduce-scatter.16.cloned.1.call-start = ((), (), s32[]{:S(2)}) async-start(), calls=%async_computation.19 | async-start | bytes 1179648 | tf_op jit(solution)/shard_map/reduce_scatter | solution.py:274
  793.0 281.6 %reduce-scatter.20.cloned.1.call-start = ((), (), s32[]{:S(2)}) async-start(), calls=%async_computation.21 | async-start | bytes 9437184 | tf_op jit(solution)/shard_map/reduce_scatter | solution.py:274
  799.3 425.4 %reduce-scatter.14.cloned.1.call-start = ((), (), s32[]{:S(2)}) async-start(), calls=%async_computation.18 | async-start | bytes 9437184 | tf_op jit(solution)/shard_map/reduce_scatter | solution.py:274
  809.1 792.1 %reduce-scatter.26.cloned.1.call-start = ((), (), s32[]{:S(2)}) async-start(), calls=%async_computation.24 | async-start | bytes 25952256 | tf_op jit(solution)/shard_map/reduce_scatter | solution.py:274
  821.8 1155.1 %reduce-scatter.24.cloned.1.call-start = ((), (), s32[]{:S(2)}) async-start(), calls=%async_computation.23 | async-start | bytes 25952256 | tf_op jit(solution)/shard_map/reduce_scatter | solution.py:274
  834.5 1518.1 %reduce-scatter.22.cloned.1.call-start = ((), (), s32[]{:S(2)}) async-start(), calls=%async_computation.22 | async-start | bytes 25952256 | tf_op jit(solution)/shard_map/reduce_scatter | solution.py:274
  847.4 1535.7 %all-reduce.15.cloned.1.call-start = ((), (), s32[]{:S(2)}) async-start(), calls=%async_computation.25 | async-start | bytes 8388608 | tf_op jit(solution)/shard_map/psum | solution.py:73
  847.4 9.4 copy-start.24
  847.4 9.4 copy-start.58
  861.0 1780.8 %all-reduce.17.cloned.1.call-start = ((), (), s32[]{:S(2)}) async-start(), calls=%async_computation.26 | async-start | bytes 22020096 | tf_op jit(solution)/shard_map/psum | solution.py:301
  2352.6 32.8 %copy-start.52 = (f32[2048]{0:T(1024)S(1)}, f32[2048]{0:T(1024)}, u32[]{:S(2)}) copy-start(f32[2048]{0:T(1024)} %get-tuple-element.44) | copy-start | bytes 24580
  2352.6 75.9 %copy-start.56 = (f32[256]{0:T(256)S(1)}, f32[256]{0:T(256)}, u32[]{:S(2)}) copy-start(f32[256]{0:T(256)} %get-tuple-element.82) | copy-start | bytes 3076
  (48 other events, 115.0 us)
Sparse Core Ops, SparseCore 0:
  10.1 86.2 all-gather.7
  98.6 72.0 all-gather.9
  175.6 19.8 all-reduce.10
  197.5 164.4 all-gather.13
  364.1 161.4 all-gather.11
  527.7 161.4 all-gather.15
  716.3 19.4 all-reduce.12
  761.9 12.9 reduce-scatter.11
  777.7 11.7 reduce-scatter.9
  793.3 64.1 reduce-scatter.17
  861.5 63.0 reduce-scatter.15
  928.1 146.3 reduce-scatter.19
  1078.2 146.5 reduce-scatter.13
  1228.5 372.7 reduce-scatter.25
  1605.0 371.8 reduce-scatter.23
  1980.6 371.8 reduce-scatter.21
  2355.5 27.5 all-reduce.14
  2386.0 255.8 all-reduce.16
where the time goes:
time: 2670 us; the launch traced here: 2660 us
  waiting for transfers between devices  2270 us (85%)
  blocking collectives  160 us (6%)
  matrix products  144 us (5%)
  other arithmetic  35.2 us (1%)
  local copies, waits for them, and re-layouts  30.6 us (1%)
    reduce_scatter x7, waiting for transfers between devices, body(): lax.psum_scatter((jnp.sum(grad_normed_one * scaled_one, axis=0), contract...  1490 us
    psum x1, waiting for transfers between devices, body(): lax.psum((gain_one_grad, query_grad, key_grad, value_grad, output_grad, g...  208 us
    all_gather x1, waiting for transfers between devices, body(): lax.all_gather(up_weight, 'fsdp', axis=0, tiled=True)  162 us
    all_gather x1, waiting for transfers between devices, body(): lax.all_gather(down_weight, 'fsdp', axis=0, tiled=True)  154 us
    all_gather x1, waiting for transfers between devices, body(): lax.all_gather(gate_weight, 'fsdp', axis=0, tiled=True)  154 us
  transfers between devices with their start and end apart: 18, of which 15 were waited for; matrix products, arithmetic and copies ran while one was open for 5% of the time, Pallas kernels for 0%

commit v1 on v0

--- a/solution.py
+++ b/solution.py
@@ -8,6 +8,27 @@
 HEAD_DIM = 64
 EPSILON = 1e-05
 NEG_FILL = -1e30
+
+
+def gather_around(array, axis, dim):
+    devices, mine, rows = (lax.axis_size(axis), lax.axis_index(axis), array.shape[dim])
+    right = [(i, (i + 1) % devices) for i in range(devices)]
+    behind = [(i, (i - 1) % devices) for i in range(devices)]
+    result = jnp.zeros((*array.shape[:dim], devices * rows, *array.shape[dim + 1 :]), array.dtype)
+    result = lax.dynamic_update_slice_in_dim(result, array, mine * rows, axis=dim)
+    from_left = from_right = array
+    half = devices // 2
+    for step in range(1, half + 1):
+        from_left = lax.ppermute(from_left, axis, right)
+        result = lax.dynamic_update_slice_in_dim(
+            result, from_left, (mine - step) % devices * rows, axis=dim
+        )
+        if step < devices - half:
+            from_right = lax.ppermute(from_right, axis, behind)
+            result = lax.dynamic_update_slice_in_dim(
+                result, from_right, (mine + step) % devices * rows, axis=dim
+            )
+    return result
 
 
 def rotary_tables(positions):
@@ -167,7 +188,7 @@
         (
             lax.all_gather(mlp_gain, "fsdp", axis=0, tiled=True),
             lax.all_gather(gate_weight, "fsdp", axis=0, tiled=True),
-            lax.all_gather(up_weight, "fsdp", axis=0, tiled=True),
+            gather_around(up_weight, "fsdp", 0),
         ),
     )
     silu_value = gate_lin / (1.0 + jnp.exp(-gate_lin))

time: 2670 us -> 2770 us (1.037)
  blocking collectives: 160 us -> 216 us
    ppermute x0 -> x7, waiting for transfers between devices: none -> 199 us  [the longest x4 156 us: gather_around(): from_left = lax.ppermute(from_left, axis, right)]
    all_gather x1, waiting for transfers between devices: 154 us -> 0.01 us  [body(): lax.all_gather(down_weight, 'fsdp', axis=0, tiled=True)]
    all_gather x1, blocking collectives: 18.3 us -> 74.3 us  [body(): lax.all_gather(mlp_gain, 'fsdp', axis=0, tiled=True)]
  transfers between devices with their start and end apart: 18 -> 25, of which waited for: 15 -> 17; matrix products, arithmetic and copies ran while one was open for 5% -> 6% of each run, Pallas kernels for 0% -> 0%
where the time goes in v1:
time: 2770 us; the launch traced here: 2760 us
  waiting for transfers between devices  2280 us (82%)
  blocking collectives  216 us (8%)
  matrix products  135 us (5%)
  local copies, waits for them, and re-layouts  52.3 us (2%)
  other arithmetic  30.8 us (1%)
    reduce_scatter x7, waiting for transfers between devices, body(): lax.psum_scatter((jnp.sum(grad_normed_one * scaled_one, axis=0), contract...  1490 us
    psum x1, waiting for transfers between devices, body(): lax.psum((gain_one_grad, query_grad, key_grad, value_grad, output_grad, g...  208 us
    ppermute x4, waiting for transfers between devices, gather_around(): from_left = lax.ppermute(from_left, axis, right)  156 us
    all_gather x1, waiting for transfers between devices, body(): lax.all_gather(gate_weight, 'fsdp', axis=0, tiled=True)  142 us
    all_gather x1, waiting for transfers between devices, body(): lax.all_gather(up_weight, 'fsdp', axis=0, tiled=True)  140 us
    all_gather x1, blocking collectives, body(): lax.all_gather(mlp_gain, 'fsdp', axis=0, tiled=True)  74.3 us
  transfers between devices with their start and end apart: 25, of which 17 were waited for; matrix products, arithmetic and copies ran while one was open for 6% of the time, Pallas kernels for 0%

profile of v1, /device:TPU:0, one launch (start us, length us, event | category | flops | bytes accessed | tf_op | source)
XLA Modules:
  0.0 2757.2 jit_solution(8583999005342605643)
XLA Ops:
  9.4 22.6 all-gather
  34.4 33.6 %all_gather.42 = bf16[2048,128]{1,0:T(8,128)(2,1)S(1)} all-gather(bf16[256,128]{1,0:T(8,128)(2,1)S(1)} %copy-done.45), channel_id=1, replica_groups=mesh['fsdp'=8,'ctx'=2,'tp'=2] {'fsdp'}, dimensions={0}, use_global_device_ids=true | all-gather | bytes 589824 | tf_op jit(solution)/shard_map/all_gather | solution.py:126
  73.7 32.5 %all_gather.40 = bf16[2048,128]{1,0:T(8,128)(2,1)S(1)} all-gather(bf16[256,128]{1,0:T(8,128)(2,1)S(1)} %copy-done.46), channel_id=1, replica_groups=mesh['fsdp'=8,'ctx'=2,'tp'=2] {'fsdp'}, dimensions={0}, use_global_device_ids=true | all-gather | bytes 589824 | tf_op jit(solution)/shard_map/all_gather | solution.py:127
  129.8 41.0 %all-gather.10.cloned.1.call-done = bf16[2048,1024]{1,0:T(8,128)(2,1)} async-done(((bf16[256,1024]{1,0:T(8,128)(2,1)}), bf16[2048,1024]{1,0:T(8,128)(2,1)}) %all-gather.10.cloned.1.call-update) | async-done | bytes 4194320 | tf_op jit(solution)/shard_map/all_gather | solution.py:181
  182.3 71.8 %collective-permute-done = bf16[256,2816]{1,0:T(8,128)(2,1)S(1)} collective-permute-done((bf16[256,2816]{1,0:T(8,128)(2,1)S(1)}, bf16[256,2816]{1,0:T(8,128)(2,1)S(1)}, u32[]{:S(2)}, u32[]{:S(2)}) %collective-permute-start) | collective-permute-done | bytes 1441824 | tf_op jit(solution)/shard_map/ppermute | solution.py:22
  260.2 84.5 %collective-permute-done.2 = bf16[256,2816]{1,0:T(8,128)(2,1)} collective-permute-done((bf16[256,2816]{1,0:T(8,128)(2,1)S(1)}, bf16[256,2816]{1,0:T(8,128)(2,1)}, u32[]{:S(2)}, u32[]{:S(2)}) %collective-permute-start.2) | collective-permute-done | bytes 1441824 | tf_op jit(solution)/shard_map/ppermute | solution.py:22
  347.3 74.3 %all-gather.1 = bf16[8,1,256]{2,1,0:T(2,128)(2,1)S(1)} all-gather(bf16[1,1,256]{2,1,0:T(2,128)(2,1)S(1)} %reshape.192), channel_id=1, replica_groups=mesh['fsdp'=8,'ctx'=2,'tp'=2] {'fsdp'}, dimensions={0}, use_global_device_ids=true | all-gather | bytes 4608 | tf_op jit(solution)/shard_map/all_gather | solution.py:189
  442.1 42.7 %collective-permute-done.5 = bf16[256,2816]{1,0:T(8,128)(2,1)S(1)} collective-permute-done((bf16[256,2816]{1,0:T(8,128)(2,1)}, bf16[256,2816]{1,0:T(8,128)(2,1)S(1)}, u32[]{:S(2)}, u32[]{:S(2)}) %collective-permute-start.5) | collective-permute-done | bytes 1441824 | tf_op jit(solution)/shard_map/ppermute | solution.py:27
  491.9 9.3 fusion.75
  501.2 141.6 %all-gather.12.cloned.1.call-done = bf16[2048,2816]{1,0:T(8,128)(2,1)} async-done(((bf16[256,2816]{1,0:T(8,128)(2,1)}), bf16[2048,2816]{1,0:T(8,128)(2,1)}) %all-gather.12.cloned.1.call-update) | async-done | bytes 11534352 | tf_op jit(solution)/shard_map/all_gather | solution.py:190
  642.8 6.7 fusion.73
  649.5 11.6 multiply_convert_fusion
  666.7 139.6 %all-gather.16.cloned.1.call-done = bf16[2048,2816]{1,0:T(8,128)(2,1)} async-done(((bf16[256,2816]{1,0:T(8,128)(2,1)}), bf16[2048,2816]{1,0:T(8,128)(2,1)}) %all-gather.16.cloned.1.call-update) | async-done | bytes 11534352 | tf_op jit(solution)/shard_map/all_gather | solution.py:212
  806.3 9.8 convolution_add_fusion.2
  816.1 8.5 reduce-scatter.10.cloned.1.call-start
  827.3 8.4 all-reduce.13.cloned.1.call-done
  863.0 7.9 reduce-scatter.10.cloned.1.call-done
  875.1 10.4 reduce-scatter.12.cloned.1.call-done
  897.2 6.3 fusion.40
  903.6 12.7 fusion.78
  916.4 12.6 fusion.79
  929.1 12.6 convolution_bitcast_fusion
  942.0 9.4 fusion.74
  955.7 65.2 %reduce-scatter.18.cloned.1.call-done = f32[256,128]{1,0:T(8,128)} async-done(((f32[2048,128]{1,0:T(8,128)}), f32[256,128]{1,0:T(8,128)}) %reduce-scatter.18.cloned.1.call-update) | async-done | bytes 131088 | tf_op jit(solution)/shard_map/reduce_scatter | solution.py:295
  1020.9 150.0 %reduce-scatter.14.cloned.1.call-done = f32[256,1024]{1,0:T(8,128)} async-done(((f32[2048,1024]{1,0:T(8,128)}), f32[256,1024]{1,0:T(8,128)}) %reduce-scatter.14.cloned.1.call-update) | async-done | bytes 1048592 | tf_op jit(solution)/shard_map/reduce_scatter | solution.py:295
  1170.9 150.2 %reduce-scatter.20.cloned.1.call-done = f32[256,1024]{1,0:T(8,128)} async-done(((f32[2048,1024]{1,0:T(8,128)}), f32[256,1024]{1,0:T(8,128)}) %reduce-scatter.20.cloned.1.call-update) | async-done | bytes 1048592 | tf_op jit(solution)/shard_map/reduce_scatter | solution.py:295
  1321.1 375.9 %reduce-scatter.22.cloned.1.call-done = f32[256,2816]{1,0:T(8,128)} async-done(((f32[2048,2816]{1,0:T(8,128)}), f32[256,2816]{1,0:T(8,128)}) %reduce-scatter.22.cloned.1.call-update) | async-done | bytes 2883600 | tf_op jit(solution)/shard_map/reduce_scatter | solution.py:295
  1697.0 375.9 %reduce-scatter.24.cloned.1.call-done = f32[256,2816]{1,0:T(8,128)} async-done(((f32[2048,2816]{1,0:T(8,128)}), f32[256,2816]{1,0:T(8,128)}) %reduce-scatter.24.cloned.1.call-update) | async-done | bytes 2883600 | tf_op jit(solution)/shard_map/reduce_scatter | solution.py:295
  2073.0 376.5 %reduce-scatter.26.cloned.1.call-done = f32[256,2816]{0,1:T(8,128)} async-done(((f32[2048,2816]{0,1:T(8,128)}), f32[256,2816]{0,1:T(8,128)}) %reduce-scatter.26.cloned.1.call-update) | async-done | bytes 2883600 | tf_op jit(solution)/shard_map/reduce_scatter | solution.py:295
  2451.3 28.6 %all-reduce.15.cloned.1.call-done = (f32[256,2048]{1,0:T(8,128)}, f32[256,2048]{1,0:T(8,128)}) async-done(((f32[256,2048]{1,0:T(8,128)}, f32[256,2048]{1,0:T(8,128)}), (f32[256,2048]{1,0:T(8,128)}, f32[256,2048]{1,0:T(8,128)})) %all-reduce.15.cloned.1.call-update) | async-done | bytes 4194320 | tf_op jit(solution)/shard_map/psum | solution.py:94
  2482.2 37.3 %all-reduce.2 = (f32[2048]{0:T(1024)S(1)}, f32[2048]{0:T(1024)S(1)}) all-reduce(f32[2048]{0:T(1024)S(1)} %get-tuple-element.46, f32[2048]{0:T(1024)S(1)} %copy-done.51), channel_id=4, replica_groups=mesh['fsdp'=8,'ctx'=2,'tp'=2] {'fsdp'}, use_global_device_ids=true, to_apply=%region_17.18.clone | all-reduce | flops 4096 | bytes 32768
  2530.5 208.2 %all-reduce.17.cloned.1.call-done = (f32[256,1024]{1,0:T(8,128)}, f32[256,128]{1,0:T(8,128)}, f32[256,128]{1,0:T(8,128)}, f32[256,1024]{1,0:T(8,128)}, f32[256,2...) async-done(((f32[256,1024]{1,0:T(8,128)}, f32[256,128]{1,0:T(8,128)}, f32[256,128]{1,0:T(8,128)}, f32[256,1024]{1,0:T(8,128)}, f32[256,2816]{1,0:T(8,128)}, ...) | async-done | bytes 11010064 | tf_op jit(solution)/shard_map/psum | solution.py:322
  (279 shorter events, 162.5 us)
Async XLA Ops:
  7.2 105.3 %all-gather.8.cloned.1.call-start = ((), (), s32[]{:S(2)}) async-start(), calls=%async_computation.9 | async-start | bytes 4718592 | tf_op jit(solution)/shard_map/all_gather | solution.py:125
  7.9 162.9 %all-gather.10.cloned.1.call-start = ((), (), s32[]{:S(2)}) async-start(), calls=%async_computation.10 | async-start | bytes 4718592 | tf_op jit(solution)/shard_map/all_gather | solution.py:181
  8.7 478.6 %all-reduce.11.cloned.1.call-start = ((), (), s32[]{:S(2)}) async-start(), calls=%async_computation.11 | async-start | bytes 4194304 | tf_op jit(solution)/shard_map/psum | solution.py:94
  33.8 39.9 %copy-start.46 = (bf16[256,128]{1,0:T(8,128)(2,1)S(1)}, bf16[256,128]{1,0:T(8,128)(2,1)}, u32[]{:S(2)}) copy-start(bf16[256,128]{1,0:T(8,128)(2,1)} %param.17) | copy-start | bytes 196612
  34.4 78.1 %copy-start.47 = (f32[256]{0:T(256)}, f32[256]{0:T(256)S(1)}, u32[]{:S(2)}) copy-start(f32[256]{0:T(256)S(1)} %get-tuple-element.83) | copy-start | bytes 3076
  68.0 38.7 %copy-start.20 = (bf16[2048,128]{1,0:T(8,128)(2,1)}, bf16[2048,128]{1,0:T(8,128)(2,1)S(1)}, u32[]{:S(2)}) copy-start(bf16[2048,128]{1,0:T(8,128)(2,1)S(1)} %all_gather.42) | copy-start | bytes 1572868
  129.0 41.9 %copy-start.37 = (bf16[64,8,256]{2,0,1:T(8,128)(2,1)}, bf16[64,8,256]{2,0,1:T(8,128)(2,1)S(1)}, u32[]{:S(2)}) copy-start(bf16[64,8,256]{2,0,1:T(8,128)(2,1)S(1)} %fusion.29) | copy-start | bytes 786436
  129.8 45.9 %copy-start.38 = (bf16[64,8,256]{2,0,1:T(8,128)(2,1)}, bf16[64,8,256]{2,0,1:T(8,128)(2,1)S(1)}, u32[]{:S(2)}) copy-start(bf16[64,8,256]{2,0,1:T(8,128)(2,1)S(1)} %fusion.30) | copy-start | bytes 786436
  175.7 171.6 %copy-start.58 = (bf16[256]{0:T(256)(128)(2,1)S(1)}, bf16[256]{0:T(256)(128)(2,1)}, u32[]{:S(2)}) copy-start(bf16[256]{0:T(256)(128)(2,1)} %param.19) | copy-start | bytes 1540
  175.7 316.1 %all-gather.14.cloned.1.call-start = ((), (), s32[]{:S(2)}) async-start(), calls=%async_computation.13 | async-start | bytes 12976128 | tf_op jit(solution)/shard_map/all_gather | solution.py:197
  176.3 466.5 %all-gather.12.cloned.1.call-start = ((), (), s32[]{:S(2)}) async-start(), calls=%async_computation.12 | async-start | bytes 12976128 | tf_op jit(solution)/shard_map/all_gather | solution.py:190
  176.9 629.5 %all-gather.16.cloned.1.call-start = ((), (), s32[]{:S(2)}) async-start(), calls=%async_computation.14 | async-start | bytes 12976128 | tf_op jit(solution)/shard_map/all_gather | solution.py:212
  177.5 658.3 %all-reduce.13.cloned.1.call-start = ((), (), s32[]{:S(2)}) async-start(), calls=%async_computation.15 | async-start | bytes 4194304 | tf_op jit(solution)/shard_map/psum | solution.py:94
  177.5 76.6 %collective-permute-start = (bf16[256,2816]{1,0:T(8,128)(2,1)S(1)}, bf16[256,2816]{1,0:T(8,128)(2,1)S(1)}, u32[]{:S(2)}, u32[]{:S(2)}) collective-permute-start(bf16[256,2816]{1,0:T(8,128)(2,1)S(1)} %copy-done.12), channel_id=1, source_target_pairs={{0,4},{4,8},{8,12},{12,16},{16,20},{20,24},{24,28},{28,0},{1,5},{5... | collective-permute-start | bytes 4325384 | tf_op jit(solution)/shard_map/ppermute | solution.py:22
  178.1 78.5 %collective-permute-start.1 = (bf16[256,2816]{1,0:T(8,128)(2,1)S(1)}, bf16[256,2816]{1,0:T(8,128)(2,1)}, u32[]{:S(2)}, u32[]{:S(2)}) collective-permute-start(bf16[256,2816]{1,0:T(8,128)(2,1)S(1)} %copy-done.12), channel_id=1, source_target_pairs={{0,28},{4,0},{8,4},{12,8},{16,12},{20,16},{24,20},{28,24},{1,29},{... | collective-permute-start | bytes 4325384 | tf_op jit(solution)/shard_map/ppermute | solution.py:27
  254.1 90.6 %collective-permute-start.2 = (bf16[256,2816]{1,0:T(8,128)(2,1)S(1)}, bf16[256,2816]{1,0:T(8,128)(2,1)}, u32[]{:S(2)}, u32[]{:S(2)}) collective-permute-start(bf16[256,2816]{1,0:T(8,128)(2,1)S(1)} %collective-permute-done), channel_id=1, source_target_pairs={{0,4},{4,8},{8,12},{12,16},{16,20},{20,24},{24,28},{28,0},{1,5},{5... | collective-permute-start | bytes 4325384 | tf_op jit(solution)/shard_map/ppermute | solution.py:22
  256.6 173.2 %collective-permute-start.3 = (bf16[256,2816]{1,0:T(8,128)(2,1)}, bf16[256,2816]{1,0:T(8,128)(2,1)}, u32[]{:S(2)}, u32[]{:S(2)}) collective-permute-start(bf16[256,2816]{1,0:T(8,128)(2,1)} %collective-permute-done.1), channel_id=1, source_target_pairs={{0,28},{4,0},{8,4},{12,8},{16,12},{20,16},{24,20},{28,24},{1,29},{... | collective-permute-start | bytes 4325384 | tf_op jit(solution)/shard_map/ppermute | solution.py:27
  344.7 87.6 %collective-permute-start.4 = (bf16[256,2816]{1,0:T(8,128)(2,1)}, bf16[256,2816]{1,0:T(8,128)(2,1)}, u32[]{:S(2)}, u32[]{:S(2)}) collective-permute-start(bf16[256,2816]{1,0:T(8,128)(2,1)} %collective-permute-done.2), channel_id=1, source_target_pairs={{0,4},{4,8},{8,12},{12,16},{16,20},{20,24},{24,28},{28,0},{1,5},{5... | collective-permute-start | bytes 4325384 | tf_op jit(solution)/shard_map/ppermute | solution.py:22
  429.7 55.0 %collective-permute-start.5 = (bf16[256,2816]{1,0:T(8,128)(2,1)}, bf16[256,2816]{1,0:T(8,128)(2,1)S(1)}, u32[]{:S(2)}, u32[]{:S(2)}) collective-permute-start(bf16[256,2816]{1,0:T(8,128)(2,1)} %collective-permute-done.3), channel_id=1, source_target_pairs={{0,28},{4,0},{8,4},{12,8},{16,12},{20,16},{24,20},{28,24},{1,29},{... | collective-permute-start | bytes 4325384 | tf_op jit(solution)/shard_map/ppermute | solution.py:27
  432.3 53.7 %collective-permute-start.6 = (bf16[256,2816]{1,0:T(8,128)(2,1)}, bf16[256,2816]{1,0:T(8,128)(2,1)S(1)}, u32[]{:S(2)}, u32[]{:S(2)}) collective-permute-start(bf16[256,2816]{1,0:T(8,128)(2,1)} %collective-permute-done.4), channel_id=1, source_target_pairs={{0,4},{4,8},{8,12},{12,16},{16,20},{20,24},{24,28},{28,0},{1,5},{5... | collective-permute-start | bytes 4325384 | tf_op jit(solution)/shard_map/ppermute | solution.py:22
  816.1 54.8 %reduce-scatter.10.cloned.1.call-start = ((), (), s32[]{:S(2)}) async-start(), calls=%async_computation.16 | async-start | bytes 393216 | tf_op jit(solution)/shard_map/reduce_scatter | solution.py:259
  857.8 27.7 %reduce-scatter.12.cloned.1.call-start = ((), (), s32[]{:S(2)}) async-start(), calls=%async_computation.17 | async-start | bytes 393216 | tf_op jit(solution)/shard_map/reduce_scatter | solution.py:262
  863.0 92.7 %reduce-scatter.16.cloned.1.call-start = ((), (), s32[]{:S(2)}) async-start(), calls=%async_computation.19 | async-start | bytes 1179648 | tf_op jit(solution)/shard_map/reduce_scatter | solution.py:295
  875.1 145.9 %reduce-scatter.18.cloned.1.call-start = ((), (), s32[]{:S(2)}) async-start(), calls=%async_computation.20 | async-start | bytes 1179648 | tf_op jit(solution)/shard_map/reduce_scatter | solution.py:295
  888.0 282.9 %reduce-scatter.14.cloned.1.call-start = ((), (), s32[]{:S(2)}) async-start(), calls=%async_computation.18 | async-start | bytes 9437184 | tf_op jit(solution)/shard_map/reduce_scatter | solution.py:295
  896.9 424.2 %reduce-scatter.20.cloned.1.call-start = ((), (), s32[]{:S(2)}) async-start(), calls=%async_computation.21 | async-start | bytes 9437184 | tf_op jit(solution)/shard_map/reduce_scatter | solution.py:295
  903.6 793.5 %reduce-scatter.22.cloned.1.call-start = ((), (), s32[]{:S(2)}) async-start(), calls=%async_computation.22 | async-start | bytes 25952256 | tf_op jit(solution)/shard_map/reduce_scatter | solution.py:295
  916.4 1156.6 %reduce-scatter.24.cloned.1.call-start = ((), (), s32[]{:S(2)}) async-start(), calls=%async_computation.23 | async-start | bytes 25952256 | tf_op jit(solution)/shard_map/reduce_scatter | solution.py:295
  929.0 1520.4 %reduce-scatter.26.cloned.1.call-start = ((), (), s32[]{:S(2)}) async-start(), calls=%async_computation.24 | async-start | bytes 25952256 | tf_op jit(solution)/shard_map/reduce_scatter | solution.py:295
  941.7 1538.2 %all-reduce.15.cloned.1.call-start = ((), (), s32[]{:S(2)}) async-start(), calls=%async_computation.25 | async-start | bytes 8388608 | tf_op jit(solution)/shard_map/psum | solution.py:94
  955.6 1783.1 %all-reduce.17.cloned.1.call-start = ((), (), s32[]{:S(2)}) async-start(), calls=%async_computation.26 | async-start | bytes 22020096 | tf_op jit(solution)/shard_map/psum | solution.py:322
  2449.5 75.9 %copy-start.54 = (f32[256]{0:T(256)S(1)}, f32[256]{0:T(256)}, u32[]{:S(2)}) copy-start(f32[256]{0:T(256)} %get-tuple-element.82) | copy-start | bytes 3076
  (57 other events, 265.0 us)
Sparse Core Ops, SparseCore 0:
  10.1 86.6 all-gather.7
  98.9 71.9 all-gather.9
  175.8 19.8 all-reduce.10
  197.7 265.4 all-gather.13
  465.2 177.4 all-gather.11
  644.8 161.4 all-gather.15
  816.3 19.4 all-reduce.12
  857.9 12.9 reduce-scatter.9
  873.7 11.7 reduce-scatter.11
  889.3 64.2 reduce-scatter.15
  957.6 63.2 reduce-scatter.17
  1024.4 146.4 reduce-scatter.13
  1174.5 146.5 reduce-scatter.19
  1324.9 372.1 reduce-scatter.21
  1700.8 372.1 reduce-scatter.23
  2076.7 372.6 reduce-scatter.25
  2452.4 27.4 all-reduce.14
  2482.8 255.8 all-reduce.16
